TPU v7x, 128 devices: a whole 4x4x4 slice. The times are simulated.
128 devices in a mesh: dp: 16 (over x, y), expert: 8 (over z, core).
Axes of the slice: x: 4, y: 4, z: 4, core: 2. Of those that a mesh axis runs over, the one named last changes fastest.
Arguments:
- layer_input: bfloat16 [16384, 2560], P(('dp', 'expert')), may hold values from -6 to 6
- output_grad: bfloat16 [16384, 2560], P(('dp', 'expert')), may hold values from -6 to 6
- expert_ids: int32 [16384, 2], P(('dp', 'expert')), may hold values from 0 to 7, all different within a row; in each aligned block of 128 rows (0 to 127, 128 to 255, ...) at most 48 rows name the same one
- gate_probs: bfloat16 [16384, 2], P(('dp', 'expert')), may hold values from 0.099609375 to 0.59765625
- gate_weight: float32 [8, 2560, 1536], P('expert', 'dp'), may hold values from -0.125 to 0.125
- up_weight: float32 [8, 2560, 1536], P('expert', 'dp'), may hold values from -0.125 to 0.125
- down_weight: float32 [8, 1536, 2560], P('expert', 'dp'), may hold values from -0.15625 to 0.15625
- gate_moment: float32 [8, 2560, 1536], P('expert', 'dp'), may hold values from -12 to 12
- up_moment: float32 [8, 2560, 1536], P('expert', 'dp'), may hold values from -12 to 12
- down_moment: float32 [8, 1536, 2560], P('expert', 'dp'), may hold values from -12 to 12
- gate_second: float32 [8, 2560, 1536], P('expert', 'dp'), may hold values from 1 to 100
- up_second: float32 [8, 2560, 1536], P('expert', 'dp'), may hold values from 1 to 100
- down_second: float32 [8, 1536, 2560], P('expert', 'dp'), may hold values from 1 to 100
Outputs:
- input_grad: bfloat16 [16384, 2560], P(('dp', 'expert'))
- prob_grad: bfloat16 [16384, 2], P(('dp', 'expert'))
- new_gate_weight: float32 [8, 2560, 1536], P('expert', 'dp')
- new_up_weight: float32 [8, 2560, 1536], P('expert', 'dp')
- new_down_weight: float32 [8, 1536, 2560], P('expert', 'dp')
- new_gate_moment: float32 [8, 2560, 1536], P('expert', 'dp')
- new_up_moment: float32 [8, 2560, 1536], P('expert', 'dp')
- new_down_moment: float32 [8, 1536, 2560], P('expert', 'dp')
- new_gate_second: float32 [8, 2560, 1536], P('expert', 'dp')
- new_up_second: float32 [8, 2560, 1536], P('expert', 'dp')
- new_down_second: float32 [8, 1536, 2560], P('expert', 'dp')
Inputs may be any that keep to these rules, and one draw needn't show every extreme that they name: `expert_ids`: each token names 2 different experts. Among the (token, pick) pairs of one device's 128 tokens, no expert is named more than 48 times, and in every draw some device's tokens name some expert exactly 48 times.
All inputs are finite; a program needn't handle non-finite values.
Results may differ from a plain program's by a relative error of at most 0.025.
Values may be sent and summed in bfloat16 or wider, within the bound.
No kernel may reach another device: no remote copies, remote signals or barrier semaphores. Data moves between devices by JAX's collectives and lax.ppermute only.
A program may use at most 256 MiB of HBM per device.

v0:
```python
import jax
import jax.numpy as jnp
from jax import lax
from jax.sharding import PartitionSpec as P

beta_one = 0.9
beta_two = 0.95
learn_rate = 0.003
decay_rate = 0.1
epsilon = 1e-08
correct_one = 1.0 - 2.6561398887587e-05
correct_two = 1.0 - 0.005920529220333


def slot_tables(flat_ids, expert_count, exp_dev, groups, capacity):
    onehot = (flat_ids[:, None] == jnp.arange(expert_count, dtype=jnp.int32)[None, :]).astype(
        jnp.int32
    )
    before = jnp.cumsum(onehot, axis=0) - onehot
    ranked = jnp.sum(before * onehot, axis=1)
    device = flat_ids // exp_dev
    local = flat_ids % exp_dev
    return (local * groups + device) * capacity + ranked


def adamw(weight, moment, second, grad):
    moment_new = beta_one * moment + (1.0 - beta_one) * grad
    second_new = beta_two * second + (1.0 - beta_two) * grad * grad
    update = moment_new / correct_one / (jnp.sqrt(second_new / correct_two) + epsilon)
    return (weight - learn_rate * (update + decay_rate * weight), moment_new, second_new)


def body(
    layer_input,
    output_grad,
    expert_ids,
    gate_probs,
    gate_weight,
    up_weight,
    down_weight,
    gate_moment,
    up_moment,
    down_moment,
    gate_second,
    up_second,
    down_second,
):
    exp_dev = gate_weight.shape[0]
    hidden_units = gate_weight.shape[2]
    width = layer_input.shape[1]
    groups = lax.axis_size("expert")
    tok_count, picks = expert_ids.shape
    capacity = 3 * tok_count * picks // (2 * exp_dev * groups)
    slots = exp_dev * groups * capacity
    row_count = groups * capacity
    dest_slot = slot_tables(expert_ids.reshape(-1), exp_dev * groups, exp_dev, groups, capacity)
    owner = (
        jnp.zeros((slots,), jnp.int32)
        .at[dest_slot]
        .set(jnp.arange(tok_count * picks, dtype=jnp.int32) // picks)
    )
    filled = jnp.zeros((slots,), jnp.int32).at[dest_slot].set(1) > 0
    zero_val = jnp.zeros((), jnp.bfloat16)
    send_input = jnp.where(filled[:, None], layer_input[owner], zero_val).reshape(
        exp_dev, groups, capacity, width
    )
    send_grad = jnp.where(filled[:, None], output_grad[owner], zero_val).reshape(
        exp_dev, groups, capacity, width
    )
    send_gate = (
        jnp.zeros((slots,), jnp.bfloat16)
        .at[dest_slot]
        .set(gate_probs.reshape(-1))
        .reshape(exp_dev, groups, capacity)
    )
    w_gate_up_shard = jnp.concatenate((gate_weight, up_weight), axis=2).astype(jnp.bfloat16)
    w_down_shard = down_weight.astype(jnp.bfloat16)
    w_gate_up, w_down = (
        lax.all_gather(w_gate_up_shard, "dp", axis=1, tiled=True),
        lax.all_gather(w_down_shard, "dp", axis=1, tiled=True),
    )
    recv_input, recv_grad, recv_gate = (
        lax.all_to_all(send_input, "expert", split_axis=1, concat_axis=1, tiled=True),
        lax.all_to_all(send_grad, "expert", split_axis=1, concat_axis=1, tiled=True),
        lax.all_to_all(send_gate, "expert", split_axis=1, concat_axis=1, tiled=True),
    )
    x_rows = recv_input.reshape(exp_dev, row_count, width)
    dy_rows = recv_grad.reshape(exp_dev, row_count, width)
    gate_rows = recv_gate.reshape(exp_dev, row_count)
    pre = jnp.einsum("erd,edf->erf", x_rows, w_gate_up, preferred_element_type=jnp.float32)
    gate_pre = pre[:, :, :hidden_units]
    up_pre = pre[:, :, hidden_units:]
    sigmoid_gate = jax.nn.sigmoid(gate_pre)
    silu_gate = gate_pre * sigmoid_gate
    hidden_full = silu_gate * up_pre
    hidden = hidden_full.astype(jnp.bfloat16)
    gate_col = gate_rows.astype(jnp.float32)[:, :, None]
    raw_grad = jnp.einsum("erd,efd->erf", dy_rows, w_down, preferred_element_type=jnp.float32)
    prob_rows = jnp.sum(hidden.astype(jnp.float32) * raw_grad, axis=2).astype(jnp.bfloat16)
    hidden_scaled = (gate_col * hidden_full).astype(jnp.bfloat16)
    hidden_grad = gate_col * raw_grad
    dsilu = sigmoid_gate * (1.0 + gate_pre * (1.0 - sigmoid_gate))
    pre_grad = jnp.concatenate(
        (hidden_grad * up_pre * dsilu, hidden_grad * silu_gate), axis=2
    ).astype(jnp.bfloat16)
    input_rows = jnp.einsum(
        "erf,edf->erd", pre_grad, w_gate_up, preferred_element_type=jnp.float32
    ).astype(jnp.bfloat16)
    second = jnp.einsum(
        "erc,erd->ecd", hidden_scaled, dy_rows, preferred_element_type=jnp.float32
    ).astype(jnp.bfloat16)
    first = jnp.einsum("erc,erf->ecf", x_rows, pre_grad, preferred_element_type=jnp.float32).astype(
        jnp.bfloat16
    )
    grad_down = lax.psum_scatter(second[0], "dp", scatter_dimension=0, tiled=True)[None].astype(
        jnp.float32
    )
    grad_gate_up = lax.psum_scatter(first[0], "dp", scatter_dimension=0, tiled=True)[None].astype(
        jnp.float32
    )
    back_input, back_prob = (
        lax.all_to_all(
            input_rows.reshape(exp_dev, groups, capacity, width),
            "expert",
            split_axis=1,
            concat_axis=1,
            tiled=True,
        ),
        lax.all_to_all(
            prob_rows.reshape(exp_dev, groups, capacity),
            "expert",
            split_axis=1,
            concat_axis=1,
            tiled=True,
        ),
    )
    picked_rows = back_input.reshape(slots, width)[dest_slot].reshape(tok_count, picks, width)
    input_grad = jnp.sum(picked_rows.astype(jnp.float32), axis=1).astype(jnp.bfloat16)
    prob_grad = back_prob.reshape(slots)[dest_slot].reshape(tok_count, picks)
    new_gate_weight, new_gate_moment, new_gate_second = adamw(
        gate_weight, gate_moment, gate_second, grad_gate_up[:, :, :hidden_units]
    )
    new_up_weight, new_up_moment, new_up_second = adamw(
        up_weight, up_moment, up_second, grad_gate_up[:, :, hidden_units:]
    )
    new_down_weight, new_down_moment, new_down_second = adamw(
        down_weight, down_moment, down_second, grad_down
    )
    return (
        input_grad,
        prob_grad,
        new_gate_weight,
        new_up_weight,
        new_down_weight,
        new_gate_moment,
        new_up_moment,
        new_down_moment,
        new_gate_second,
        new_up_second,
        new_down_second,
    )


def solution(mesh):
    return jax.shard_map(
        body,
        mesh=mesh,
        in_specs=(
            P(("dp", "expert"), None),
            P(("dp", "expert"), None),
            P(("dp", "expert"), None),
            P(("dp", "expert"), None),
            P("expert", "dp", None),
            P("expert", "dp", None),
            P("expert", "dp", None),
            P("expert", "dp", None),
            P("expert", "dp", None),
            P("expert", "dp", None),
            P("expert", "dp", None),
            P("expert", "dp", None),
            P("expert", "dp", None),
        ),
        out_specs=(
            P(("dp", "expert"), None),
            P(("dp", "expert"), None),
            P("expert", "dp", None),
            P("expert", "dp", None),
            P("expert", "dp", None),
            P("expert", "dp", None),
            P("expert", "dp", None),
            P("expert", "dp", None),
            P("expert", "dp", None),
            P("expert", "dp", None),
            P("expert", "dp", None),
        ),
        check_vma=False,
    )
```

profile of v0, /device:TPU:1, one launch (start us, length us, event | category | flops | bytes accessed | tf_op | source)
XLA Modules:
  0.0 440.1 jit_solution(14314940471210939129)
XLA Ops:
  7.2 1.3 convert.18
  8.6 1.3 convert.17
  9.8 1.0 pad_maximum_fusion.3
  12.8 2.2 scatter_custom_fusion
  15.7 6.8 %all-to-all-start = ((bf16[1,8,48]{2,0,1:T(2,128)(2,1)}), bf16[1,8,48]{2,0,1:T(2,128)(2,1)S(1)}, u32[]{:S(2)}, u32[]{:S(2)}) async-start(bf16[1,8,48]{2,0,1:T(2,128)(2,1)} %reshape.315), calls=%async_computation | async-start | bytes 8192 | tf_op jit(solution)/shard_map/all_to_all | solution.py:85
  22.5 1.4 scatter_custom_fusion.2
  23.9 1.4 scatter_custom_fusion.1
  25.5 3.3 gather_fusion.1
  28.8 3.3 gather_fusion
  32.0 3.8 broadcast_select_fusion
  35.9 29.9 %all_to_all.25 = bf16[1,8,48,2560]{3,2,0,1:T(8,128)(2,1)} all-to-all(bf16[1,8,48,2560]{3,2,0,1:T(8,128)(2,1)S(1)} %get-tuple-element.60), channel_id=1, replica_groups=mesh['dp'=16,'expert'=8] {'expert'}, dimensions={1} | all-to-all | bytes 3932160 | tf_op jit(solution)/shard_map/all_to_all | solution.py:83
  65.8 5.2 %all-to-all-start.1 = ((bf16[1,8,48,2560]{3,2,0,1:T(8,128)(2,1)}), bf16[1,8,48,2560]{3,2,0,1:T(8,128)(2,1)}, u32[]{:S(2)}, u32[]{:S(2)}) async-start(bf16[1,8,48,2560]{3,2,0,1:T(8,128)(2,1)} %get-tuple-element.61), calls=%async_computation.1 | async-start | bytes 3932160 | tf_op jit(solution)/shard_map/all_to_all | solution.py:84
  71.1 49.0 %all-gather.5.cloned.1.call-done = bf16[1,2560,3072]{2,1,0:T(8,128)(2,1)} async-done(((bf16[1,160,3072]{2,1,0:T(8,128)(2,1)}), bf16[1,2560,3072]{2,1,0:T(8,128)(2,1)}) %all-gather.5.cloned.1.call-update) | async-done | bytes 15728656 | tf_op jit(solution)/shard_map/all_gather | solution.py:79
  120.1 12.2 %fusion.6 = f32[1,384,3072]{2,1,0:T(8,128)} fusion(bf16[384,2560]{1,0:T(8,128)(2,1)S(1)} %bitcast.82, bf16[1,2560,3072]{2,1,0:T(8,128)(2,1)} %all-gather.5.cloned.1.call-done), kind=kOutput, calls=%fused_computation.15 | convolution fusion | flops 6039797760 | bytes 22413312 | tf_op jit(solution)/shard_map/erd,edf->erf/dot_general | solution.py:90
  132.3 10.6 %convolution_convert_fusion.1 = bf16[1536,2560]{1,0:T(8,128)(2,1)} fusion(bf16[384,2560]{1,0:T(8,128)(2,1)} %bitcast.6, f32[384]{0:T(512)S(1)} %reshape.255, f32[1,384,3072]{2,1,0:T(8,128)} %fusion.6), kind=kOutput, calls=%fused_computation.12 | convolution fusion | flops 3027959808 | bytes 14550528 | tf_op jit(solution)/shard_map/erc,erd->ecd/dot_general | solution.py:109
  142.9 82.5 %reduce-scatter.5.cloned.1.call-done = bf16[96,2560]{1,0:T(8,128)(2,1)} async-done(((bf16[1536,2560]{1,0:T(8,128)(2,1)}), bf16[96,2560]{1,0:T(8,128)(2,1)}) %reduce-scatter.5.cloned.1.call-update) | async-done | bytes 491536 | tf_op jit(solution)/shard_map/reduce_scatter | solution.py:115
  225.4 4.5 %multiply_subtract_fusion = (f32[1,96,2560]{2,1,0:T(8,128)}, f32[1,96,2560]{2,1,0:T(8,128)}, f32[1,96,2560]{2,1,0:T(8,128)}, bf16[1,96,2560]{2,1,0:T(8,128)(2,1)}) fusion(f32[1,96,2560]{2,1,0:T(8,128)} %param.19, bf16[96,2560]{1,0:T(8,128)(2,1)} %reduce-scatter.5.cloned.1.call-done, f32[1,96,2560]{2,1,0:T(8,128)} %param.22, f32[1,96,2560]{2,1,0:T(8,128)} %param.25), kind=kLoop, calls=%fused_computation.47 | loop fusion | flops 4177920 | bytes 6881280 | tf_op jit(solution)/shard_map/sub | solution.py:30
  230.2 68.9 %all-gather.3.cloned.1.call-done = bf16[1,1536,2560]{2,1,0:T(8,128)(2,1)} async-done(((bf16[1,96,2560]{2,1,0:T(8,128)(2,1)}), bf16[1,1536,2560]{2,1,0:T(8,128)(2,1)}) %all-gather.3.cloned.1.call-update) | async-done | bytes 7864336 | tf_op jit(solution)/shard_map/all_gather | solution.py:80
  299.1 9.1 %fusion.21 = (bf16[384,1536]{1,0:T(8,128)(2,1)S(1)}, bf16[384,1536]{1,0:T(8,128)(2,1)S(1)}, bf16[384]{0:T(512)(128)(2,1)S(1)}) fusion(f32[1,384,3072]{2,1,0:T(8,128)} %fusion.6, f32[384]{0:T(512)S(1)} %reshape.255, bf16[384,2560]{1,0:T(8,128)(2,1)} %bitcast.6, bf16[1,1536,2560]{2,1,0:T(8,128)(2,1)} %all-gather.3.cloned.1.call-done), kind=kOutput, calls=%fused_computation.38 | convolution fusion | flops 3031105024 | bytes 16910592 | tf_op jit(solution)/shard_map/erd,efd->erf/dot_general | solution.py:98
  308.3 1.0 copy-done.8
  309.7 11.5 %convolution_convert_fusion = bf16[2560,3072]{1,0:T(8,128)(2,1)} fusion(bf16[384,2560]{1,0:T(8,128)(2,1)S(1)} %bitcast.83, bf16[384,1536]{1,0:T(8,128)(2,1)S(1)} %get-tuple-element.54, bf16[384,1536]{1,0:T(8,128)(2,1)S(1)} %get-tuple-element.53), kind=kOutput, calls=%fused_computation.7 | convolution fusion | flops 6052380672 | bytes 20054016 | tf_op jit(solution)/shard_map/erc,erf->ecf/dot_general | solution.py:112
  321.9 5.1 %all-to-all-start.4 = ((bf16[1,8,48]{2,0,1:T(2,128)(2,1)}), bf16[1,8,48]{2,0,1:T(2,128)(2,1)S(1)}, u32[]{:S(2)}, u32[]{:S(2)}) async-start(bf16[1,8,48]{2,0,1:T(2,128)(2,1)} %convert_element_type.102), calls=%async_computation.4 | async-start | bytes 8192 | tf_op jit(solution)/shard_map/all_to_all | solution.py:129
  327.0 11.0 %fusion.9 = bf16[384,2560]{1,0:T(8,128)(2,1)} fusion(bf16[1,2560,3072]{2,1,0:T(8,128)(2,1)} %all-gather.5.cloned.1.call-done, bf16[384,1536]{1,0:T(8,128)(2,1)} %copy-done.10, bf16[384,1536]{1,0:T(8,128)(2,1)S(1)} %copy-done.9), kind=kOutput, calls=%fused_computation.16 | convolution fusion | flops 6045499392 | bytes 20054016 | tf_op jit(solution)/shard_map/erf,edf->erd/dot_general | solution.py:106
  338.0 4.8 %all-to-all-start.3 = ((bf16[1,8,48,2560]{3,2,0,1:T(8,128)(2,1)}), bf16[1,8,48,2560]{3,2,0,1:T(8,128)(2,1)S(1)}, u32[]{:S(2)}, u32[]{:S(2)}) async-start(bf16[1,8,48,2560]{3,2,0,1:T(8,128)(2,1)} %bitcast.84), calls=%async_computation.3 | async-start | bytes 3932160 | tf_op jit(solution)/shard_map/all_to_all | solution.py:122
  342.9 1.9 gather_fusion.3
  345.6 22.1 %all-to-all-done.3 = bf16[1,8,48,2560]{3,2,0,1:T(8,128)(2,1)S(1)} async-done(((bf16[1,8,48,2560]{3,2,0,1:T(8,128)(2,1)}), bf16[1,8,48,2560]{3,2,0,1:T(8,128)(2,1)S(1)}, u32[]{:S(2)}, u32[]{:S(2)}) %all-to-all-start.3) | async-done | bytes 1966112 | tf_op jit(solution)/shard_map/all_to_all | solution.py:122
  367.7 2.5 gather_fusion.2
  370.3 3.1 reshape.251
  373.4 4.4 reduce_sum.34
  377.7 48.6 %reduce-scatter.3.cloned.1.call-done = bf16[160,3072]{1,0:T(8,128)(2,1)} async-done(((bf16[2560,3072]{1,0:T(8,128)(2,1)}), bf16[160,3072]{1,0:T(8,128)(2,1)}) %reduce-scatter.3.cloned.1.call-update) | async-done | bytes 983056 | tf_op jit(solution)/shard_map/reduce_scatter | solution.py:118
  426.3 1.4 bitcast_convert_fusion
  427.8 5.8 %multiply_subtract_fusion.1 = (f32[1,160,1536]{2,1,0:T(8,128)}, f32[1,160,1536]{2,1,0:T(8,128)}, f32[1,160,1536]{2,1,0:T(8,128)}, f32[1,160,1536]{2,1,0:T(8,128)...) fusion(f32[1,160,1536]{2,1,0:T(8,128)S(1)} %copy-done.3, f32[1,160,3072]{2,1,0:T(8,128)S(1)} %bitcast_convert_fusion, ...), kind=kLoop, calls=%fused_computation.48 | loop fusion | flops 7372800 | bytes 13762560 | tf_op jit(solution)/shard_map/sub | solution.py:30
  (62 shorter events, 5.2 us)
Async XLA Ops:
  7.2 18.3 %copy-start = (bf16[128,2560]{1,0:T(8,128)(2,1)S(1)}, bf16[128,2560]{1,0:T(8,128)(2,1)}, u32[]{:S(2)}) copy-start(bf16[128,2560]{1,0:T(8,128)(2,1)} %param.13) | copy-start | bytes 1966084
  7.2 112.9 %all-gather.5.cloned.1.call-start = ((), (), s32[]{:S(2)}) async-start(), calls=%async_computation.8 | async-start | bytes 16711680 | tf_op jit(solution)/shard_map/all_gather | solution.py:79
  8.6 2.4 copy-start.6
  8.6 3.9 copy-start.7
  15.7 20.2 %all-to-all-start = ((bf16[1,8,48]{2,0,1:T(2,128)(2,1)}), bf16[1,8,48]{2,0,1:T(2,128)(2,1)S(1)}, u32[]{:S(2)}, u32[]{:S(2)}) async-start(bf16[1,8,48]{2,0,1:T(2,128)(2,1)} %reshape.315), calls=%async_computation | async-start | bytes 8192 | tf_op jit(solution)/shard_map/all_to_all | solution.py:85
  25.5 3.3 copy-start.2
  65.8 54.3 %copy-start.5 = (bf16[1,8,48,2560]{3,2,0,1:T(8,128)(2,1)S(1)}, bf16[1,8,48,2560]{3,2,0,1:T(8,128)(2,1)}, u32[]{:S(2)}) copy-start(bf16[1,8,48,2560]{3,2,0,1:T(8,128)(2,1)} %all_to_all.25) | copy-start | bytes 5898244
  65.8 66.5 %all-to-all-start.1 = ((bf16[1,8,48,2560]{3,2,0,1:T(8,128)(2,1)}), bf16[1,8,48,2560]{3,2,0,1:T(8,128)(2,1)}, u32[]{:S(2)}, u32[]{:S(2)}) async-start(bf16[1,8,48,2560]{3,2,0,1:T(8,128)(2,1)} %get-tuple-element.61), calls=%async_computation.1 | async-start | bytes 3932160 | tf_op jit(solution)/shard_map/all_to_all | solution.py:84
  71.0 154.4 %reduce-scatter.5.cloned.1.call-start = ((), (), s32[]{:S(2)}) async-start(), calls=%async_computation.10 | async-start | bytes 8355840 | tf_op jit(solution)/shard_map/reduce_scatter | solution.py:115
  142.8 156.3 %all-gather.3.cloned.1.call-start = ((), (), s32[]{:S(2)}) async-start(), calls=%async_computation.7 | async-start | bytes 8355840 | tf_op jit(solution)/shard_map/all_gather | solution.py:80
  229.9 196.4 %reduce-scatter.3.cloned.1.call-start = ((), (), s32[]{:S(2)}) async-start(), calls=%async_computation.9 | async-start | bytes 16711680 | tf_op jit(solution)/shard_map/reduce_scatter | solution.py:118
  308.3 1.0 copy-start.8
  308.3 1.4 copy-start.10
  321.2 5.8 %copy-start.9 = (bf16[384,1536]{1,0:T(8,128)(2,1)S(1)}, bf16[384,1536]{1,0:T(8,128)(2,1)}, u32[]{:S(2)}) copy-start(bf16[384,1536]{1,0:T(8,128)(2,1)} %copy-done.8) | copy-start | bytes 3538948
  321.9 16.1 %all-to-all-start.4 = ((bf16[1,8,48]{2,0,1:T(2,128)(2,1)}), bf16[1,8,48]{2,0,1:T(2,128)(2,1)S(1)}, u32[]{:S(2)}, u32[]{:S(2)}) async-start(bf16[1,8,48]{2,0,1:T(2,128)(2,1)} %convert_element_type.102), calls=%async_computation.4 | async-start | bytes 8192 | tf_op jit(solution)/shard_map/all_to_all | solution.py:129
  338.0 29.7 %all-to-all-start.3 = ((bf16[1,8,48,2560]{3,2,0,1:T(8,128)(2,1)}), bf16[1,8,48,2560]{3,2,0,1:T(8,128)(2,1)S(1)}, u32[]{:S(2)}, u32[]{:S(2)}) async-start(bf16[1,8,48,2560]{3,2,0,1:T(8,128)(2,1)} %bitcast.84), calls=%async_computation.3 | async-start | bytes 3932160 | tf_op jit(solution)/shard_map/all_to_all | solution.py:122
  373.4 54.4 %copy-start.3 = (f32[1,160,1536]{2,1,0:T(8,128)S(1)}, f32[1,160,1536]{2,1,0:T(8,128)}, u32[]{:S(2)}) copy-start(f32[1,160,1536]{2,1,0:T(8,128)} %param.18) | copy-start | bytes 2949124
  377.7 50.0 %copy-start.4 = (f32[1,160,1536]{2,1,0:T(8,128)S(1)}, f32[1,160,1536]{2,1,0:T(8,128)}, u32[]{:S(2)}) copy-start(f32[1,160,1536]{2,1,0:T(8,128)} %param.17) | copy-start | bytes 2949124
  427.8 5.8 %copy-start.1 = (bf16[128,2560]{1,0:T(8,128)(2,1)S(1)}, bf16[128,2560]{1,0:T(8,128)(2,1)}, u32[]{:S(2)}) copy-start(bf16[128,2560]{1,0:T(8,128)(2,1)} %param.13) | copy-start | bytes 1966084
Sparse Core Ops, SparseCore 0:
  11.0 108.9 all-gather.4
  143.0 82.4 reduce-scatter.4
  230.1 69.0 all-gather.2
  321.3 104.9 reduce-scatter.2
where the time goes:
time: 441 us; the launch traced here: 440 us
  waiting for transfers between devices  271 us (61%)
  matrix products  54.4 us (12%)
  blocking collectives  29.9 us (7%)
  other arithmetic  24.3 us (6%)
  local copies, waits for them, and re-layouts  24.1 us (5%)
  starting transfers between devices  22.3 us (5%)
  between operations  14 us (3%)
    reduce_scatter x1, waiting for transfers between devices, body(): lax.psum_scatter(second[0], 'dp', scatter_dimension=0, tiled=True)[None]  82.5 us
    all_gather x1, waiting for transfers between devices, body(): lax.all_gather(w_down_shard, 'dp', axis=1, tiled=True)  68.9 us
    all_gather x1, waiting for transfers between devices, body(): lax.all_gather(w_gate_up_shard, 'dp', axis=1, tiled=True)  49 us
    reduce_scatter x1, waiting for transfers between devices, body(): lax.psum_scatter(first[0], 'dp', scatter_dimension=0, tiled=True)[None]  48.6 us
    all_to_all x1, blocking collectives, body(): lax.all_to_all(send_input, 'expert', split_axis=1, concat_axis=1, tiled=T...  29.9 us
    all_to_all x1, waiting for transfers between devices, body(): lax.all_to_all(input_rows.reshape(exp_dev, groups, capacity, width), 'exp...  22.1 us
    dot_general x1, matrix products, body(): jnp.einsum('erd,edf->erf', x_rows, w_gate_up, preferred_element_type=jnp....  12.2 us
    dot_general x1, matrix products, body(): jnp.einsum('erc,erf->ecf', x_rows, pre_grad, preferred_element_type=jnp.f...  11.5 us
  transfers between devices with their start and end apart: 8, of which 5 were waited for; matrix products, arithmetic and copies ran while one was open for 12% of the time, Pallas kernels for 0%

commit v1 on v0

--- a/solution.py
+++ b/solution.py
@@ -10,6 +10,13 @@
 epsilon = 1e-08
 correct_one = 1.0 - 2.6561398887587e-05
 correct_two = 1.0 - 0.005920529220333
+
+
+def swapped_in(x, axis, dim):
+    peers = lax.axis_size(axis)
+    blocks = jnp.stack([x for _ in range(peers)])
+    blocks = lax.all_to_all(blocks, axis, split_axis=0, concat_axis=0)
+    return jnp.concatenate(blocks, axis=dim)
 
 
 def slot_tables(flat_ids, expert_count, exp_dev, groups, capacity):
@@ -77,7 +84,7 @@
     w_down_shard = down_weight.astype(jnp.bfloat16)
     w_gate_up, w_down = (
         lax.all_gather(w_gate_up_shard, "dp", axis=1, tiled=True),
-        lax.all_gather(w_down_shard, "dp", axis=1, tiled=True),
+        swapped_in(w_down_shard, "dp", 1),
     )
     recv_input, recv_grad, recv_gate = (
         lax.all_to_all(send_input, "expert", split_axis=1, concat_axis=1, tiled=True),

time: 441 us -> 467 us (1.059)
  blocking collectives: 29.9 us -> 122 us
  waiting for transfers between devices: 271 us -> 204 us
    all_to_all x0 -> x1, blocking collectives: none -> 92 us  [swapped_in(): blocks = lax.all_to_all(blocks, axis, split_axis=0, concat_axis=0)]
    all_gather x1 -> x0, waiting for transfers between devices: 68.9 us -> none  [body(): lax.all_gather(w_down_shard, 'dp', axis=1, tiled=True)]
  transfers between devices with their start and end apart: 8 -> 7, of which waited for: 5 -> 4; matrix products, arithmetic and copies ran while one was open for 12% -> 12% of each run, Pallas kernels for 0% -> 0%
where the time goes in v1:
time: 467 us; the launch traced here: 466 us
  waiting for transfers between devices  204 us (44%)
  blocking collectives  122 us (26%)
  matrix products  52.3 us (11%)
  starting transfers between devices  25.2 us (5%)
  local copies, waits for them, and re-layouts  24.1 us (5%)
  other arithmetic  24.1 us (5%)
  between operations  14 us (3%)
    all_to_all x1, blocking collectives, swapped_in(): blocks = lax.all_to_all(blocks, axis, split_axis=0, concat_axis=0)  92 us
    reduce_scatter x1, waiting for transfers between devices, body(): lax.psum_scatter(second[0], 'dp', scatter_dimension=0, tiled=True)[None]  82.4 us
    reduce_scatter x1, waiting for transfers between devices, body(): lax.psum_scatter(first[0], 'dp', scatter_dimension=0, tiled=True)[None]  50 us
    all_gather x1, waiting for transfers between devices, body(): lax.all_gather(w_gate_up_shard, 'dp', axis=1, tiled=True)  49.7 us
    all_to_all x1, blocking collectives, body(): lax.all_to_all(send_input, 'expert', split_axis=1, concat_axis=1, tiled=T...  30 us
    all_to_all x1, waiting for transfers between devices, body(): lax.all_to_all(input_rows.reshape(exp_dev, groups, capacity, width), 'exp...  22.1 us
    dot_general x1, matrix products, body(): jnp.einsum('erd,edf->erf', x_rows, w_gate_up, preferred_element_type=jnp....  12.2 us
    dot_general x1, matrix products, body(): jnp.einsum('erf,edf->erd', pre_grad, w_gate_up, preferred_element_type=jn...  11.7 us
  transfers between devices with their start and end apart: 7, of which 4 were waited for; matrix products, arithmetic and copies ran while one was open for 12% of the time, Pallas kernels for 0%

profile of v1, /device:TPU:1, one launch (start us, length us, event | category | flops | bytes accessed | tf_op | source)
XLA Modules:
  0.0 466.0 jit_solution(9435151625381841355)
XLA Ops:
  7.2 1.3 convert.17
  8.6 1.3 convert.18
  9.8 1.0 pad_maximum_fusion.3
  12.8 2.2 scatter_custom_fusion
  15.7 6.8 %all-to-all-start = ((bf16[1,8,48]{2,0,1:T(2,128)(2,1)}), bf16[1,8,48]{2,0,1:T(2,128)(2,1)S(1)}, u32[]{:S(2)}, u32[]{:S(2)}) async-start(bf16[1,8,48]{2,0,1:T(2,128)(2,1)} %reshape.320), calls=%async_computation | async-start | bytes 8192 | tf_op jit(solution)/shard_map/all_to_all | solution.py:92
  22.5 1.4 scatter_custom_fusion.2
  24.0 2.6 gather_fusion.1
  26.6 3.3 gather_fusion
  29.9 1.4 scatter_custom_fusion.1
  31.4 3.8 broadcast_select_fusion
  35.2 30.0 %all_to_all.30 = bf16[1,8,48,2560]{3,2,0,1:T(8,128)(2,1)S(1)} all-to-all(bf16[1,8,48,2560]{3,2,0,1:T(8,128)(2,1)} %get-tuple-element.60), channel_id=1, replica_groups=mesh['dp'=16,'expert'=8] {'expert'}, dimensions={1} | all-to-all | bytes 3932160 | tf_op jit(solution)/shard_map/all_to_all | solution.py:90
  65.3 5.0 %all-to-all-start.1 = ((bf16[1,8,48,2560]{3,2,0,1:T(8,128)(2,1)}), bf16[1,8,48,2560]{3,2,0,1:T(8,128)(2,1)}, u32[]{:S(2)}, u32[]{:S(2)}) async-start(bf16[1,8,48,2560]{3,2,0,1:T(8,128)(2,1)} %get-tuple-element.61), calls=%async_computation.1 | async-start | bytes 3932160 | tf_op jit(solution)/shard_map/all_to_all | solution.py:91
  70.4 49.7 %all-gather.2.cloned.1.call-done = bf16[1,2560,3072]{2,1,0:T(8,128)(2,1)} async-done(((bf16[1,160,3072]{2,1,0:T(8,128)(2,1)}), bf16[1,2560,3072]{2,1,0:T(8,128)(2,1)}) %all-gather.2.cloned.1.call-update) | async-done | bytes 15728656 | tf_op jit(solution)/shard_map/all_gather | solution.py:86
  120.1 12.2 %fusion.4 = f32[1,384,3072]{2,1,0:T(8,128)} fusion(bf16[384,2560]{1,0:T(8,128)(2,1)S(1)} %bitcast.82, bf16[1,2560,3072]{2,1,0:T(8,128)(2,1)} %all-gather.2.cloned.1.call-done), kind=kOutput, calls=%fused_computation.13 | convolution fusion | flops 6039797760 | bytes 22413312 | tf_op jit(solution)/shard_map/erd,edf->erf/dot_general | solution.py:97
  132.2 10.6 %convolution_convert_fusion.1 = bf16[1536,2560]{1,0:T(8,128)(2,1)} fusion(bf16[384,2560]{1,0:T(8,128)(2,1)} %bitcast.6, f32[384]{0:T(512)S(1)} %reshape.260, f32[1,384,3072]{2,1,0:T(8,128)} %fusion.4), kind=kOutput, calls=%fused_computation.12 | convolution fusion | flops 3027959808 | bytes 14550528 | tf_op jit(solution)/shard_map/erc,erd->ecd/dot_general | solution.py:116
  142.9 82.4 %reduce-scatter.5.cloned.1.call-done = bf16[96,2560]{1,0:T(8,128)(2,1)} async-done(((bf16[1536,2560]{1,0:T(8,128)(2,1)}), bf16[96,2560]{1,0:T(8,128)(2,1)}) %reduce-scatter.5.cloned.1.call-update) | async-done | bytes 491536 | tf_op jit(solution)/shard_map/reduce_scatter | solution.py:122
  225.3 4.3 multiply_subtract_fusion
  230.4 92.0 %all_to_all.31 = bf16[16,1,96,2560]{3,2,1,0:T(8,128)(2,1)S(1)} all-to-all(bf16[16,1,96,2560]{3,2,1,0:T(8,128)(2,1)S(1)} %stack.2), channel_id=1, replica_groups=mesh['dp'=16,'expert'=8] {'dp'}, dimensions={0} | all-to-all | bytes 15728640 | tf_op jit(solution)/shard_map/all_to_all | solution.py:18
  322.4 6.5 %fusion.19 = (bf16[384,1536]{1,0:T(8,128)(2,1)S(1)}, bf16[384,1536]{1,0:T(8,128)(2,1)S(1)}, bf16[384]{0:T(512)(128)(2,1)S(1)}) fusion(f32[1,384,3072]{2,1,0:T(8,128)} %fusion.4, f32[384]{0:T(512)S(1)} %reshape.260, bf16[384,2560]{1,0:T(8,128)(2,1)} %bitcast.6, bf16[1536,2560]{1,0:T(8,128)(2,1)S(1)} %bitcast.79), kind=kOutput, calls=%fused_computation.36 | convolution fusion | flops 3031105024 | bytes 16910592 | tf_op jit(solution)/shard_map/erd,efd->erf/dot_general | solution.py:105
  328.9 1.0 copy-done.7
  330.3 11.4 %convolution_convert_fusion = bf16[2560,3072]{1,0:T(8,128)(2,1)} fusion(bf16[384,2560]{1,0:T(8,128)(2,1)S(1)} %bitcast.83, bf16[384,1536]{1,0:T(8,128)(2,1)S(1)} %get-tuple-element.54, bf16[384,1536]{1,0:T(8,128)(2,1)S(1)} %get-tuple-element.53), kind=kOutput, calls=%fused_computation.7 | convolution fusion | flops 6052380672 | bytes 20054016 | tf_op jit(solution)/shard_map/erc,erf->ecf/dot_general | solution.py:119
  342.5 8.4 %all-to-all-start.5 = ((bf16[1,8,48]{2,0,1:T(2,128)(2,1)}), bf16[1,8,48]{2,0,1:T(2,128)(2,1)S(1)}, u32[]{:S(2)}, u32[]{:S(2)}) async-start(bf16[1,8,48]{2,0,1:T(2,128)(2,1)} %convert_element_type.105), calls=%async_computation.5 | async-start | bytes 8192 | tf_op jit(solution)/shard_map/all_to_all | solution.py:136
  350.9 11.7 %fusion.7 = bf16[384,2560]{1,0:T(8,128)(2,1)} fusion(bf16[1,2560,3072]{2,1,0:T(8,128)(2,1)} %all-gather.2.cloned.1.call-done, bf16[384,1536]{1,0:T(8,128)(2,1)S(1)} %copy-done.10, bf16[384,1536]{1,0:T(8,128)(2,1)S(1)} %copy-done.8), kind=kOutput, calls=%fused_computation.14 | convolution fusion | flops 6045499392 | bytes 20054016 | tf_op jit(solution)/shard_map/erf,edf->erd/dot_general | solution.py:113
  362.5 4.8 %all-to-all-start.4 = ((bf16[1,8,48,2560]{3,2,0,1:T(8,128)(2,1)}), bf16[1,8,48,2560]{3,2,0,1:T(8,128)(2,1)S(1)}, u32[]{:S(2)}, u32[]{:S(2)}) async-start(bf16[1,8,48,2560]{3,2,0,1:T(8,128)(2,1)} %bitcast.84), calls=%async_computation.4 | async-start | bytes 3932160 | tf_op jit(solution)/shard_map/all_to_all | solution.py:129
  367.5 1.9 gather_fusion.3
  370.2 22.1 %all-to-all-done.4 = bf16[1,8,48,2560]{3,2,0,1:T(8,128)(2,1)S(1)} async-done(((bf16[1,8,48,2560]{3,2,0,1:T(8,128)(2,1)}), bf16[1,8,48,2560]{3,2,0,1:T(8,128)(2,1)S(1)}, u32[]{:S(2)}, u32[]{:S(2)}) %all-to-all-start.4) | async-done | bytes 1966112 | tf_op jit(solution)/shard_map/all_to_all | solution.py:129
  392.3 2.5 gather_fusion.2
  394.8 3.1 reshape.256
  397.9 4.4 reduce_sum.34
  402.3 50.0 %reduce-scatter.3.cloned.1.call-done = bf16[160,3072]{1,0:T(8,128)(2,1)} async-done(((bf16[2560,3072]{1,0:T(8,128)(2,1)}), bf16[160,3072]{1,0:T(8,128)(2,1)}) %reduce-scatter.3.cloned.1.call-update) | async-done | bytes 983056 | tf_op jit(solution)/shard_map/reduce_scatter | solution.py:125
  452.3 1.4 bitcast_convert_fusion
  453.7 5.8 %multiply_subtract_fusion.1 = (f32[1,160,1536]{2,1,0:T(8,128)}, f32[1,160,1536]{2,1,0:T(8,128)}, f32[1,160,1536]{2,1,0:T(8,128)}, f32[1,160,1536]{2,1,0:T(8,128)...) fusion(f32[1,160,1536]{2,1,0:T(8,128)S(1)} %copy-done.3, f32[1,160,3072]{2,1,0:T(8,128)S(1)} %bitcast_convert_fusion, ...), kind=kLoop, calls=%fused_computation.46 | loop fusion | flops 7372800 | bytes 13762560 | tf_op jit(solution)/shard_map/sub | solution.py:37
  (61 shorter events, 5.6 us)
Async XLA Ops:
  7.2 16.8 %copy-start = (bf16[128,2560]{1,0:T(8,128)(2,1)S(1)}, bf16[128,2560]{1,0:T(8,128)(2,1)}, u32[]{:S(2)}) copy-start(bf16[128,2560]{1,0:T(8,128)(2,1)} %param.13) | copy-start | bytes 1966084
  7.2 112.9 %all-gather.2.cloned.1.call-start = ((), (), s32[]{:S(2)}) async-start(), calls=%async_computation.8 | async-start | bytes 16711680 | tf_op jit(solution)/shard_map/all_gather | solution.py:86
  8.6 2.4 copy-start.5
  8.6 3.9 copy-start.6
  15.7 19.5 %all-to-all-start = ((bf16[1,8,48]{2,0,1:T(2,128)(2,1)}), bf16[1,8,48]{2,0,1:T(2,128)(2,1)S(1)}, u32[]{:S(2)}, u32[]{:S(2)}) async-start(bf16[1,8,48]{2,0,1:T(2,128)(2,1)} %reshape.320), calls=%async_computation | async-start | bytes 8192 | tf_op jit(solution)/shard_map/all_to_all | solution.py:92
  23.9 2.6 copy-start.2
  65.3 67.0 %all-to-all-start.1 = ((bf16[1,8,48,2560]{3,2,0,1:T(8,128)(2,1)}), bf16[1,8,48,2560]{3,2,0,1:T(8,128)(2,1)}, u32[]{:S(2)}, u32[]{:S(2)}) async-start(bf16[1,8,48,2560]{3,2,0,1:T(8,128)(2,1)} %get-tuple-element.61), calls=%async_computation.1 | async-start | bytes 3932160 | tf_op jit(solution)/shard_map/all_to_all | solution.py:91
  70.3 155.0 %reduce-scatter.5.cloned.1.call-start = ((), (), s32[]{:S(2)}) async-start(), calls=%async_computation.10 | async-start | bytes 8355840 | tf_op jit(solution)/shard_map/reduce_scatter | solution.py:122
  142.8 309.5 %reduce-scatter.3.cloned.1.call-start = ((), (), s32[]{:S(2)}) async-start(), calls=%async_computation.9 | async-start | bytes 16711680 | tf_op jit(solution)/shard_map/reduce_scatter | solution.py:125
  328.9 1.0 copy-start.7
  328.9 1.4 copy-start.9
  341.8 9.1 %copy-start.8 = (bf16[384,1536]{1,0:T(8,128)(2,1)S(1)}, bf16[384,1536]{1,0:T(8,128)(2,1)}, u32[]{:S(2)}) copy-start(bf16[384,1536]{1,0:T(8,128)(2,1)} %copy-done.7) | copy-start | bytes 3538948
  341.8 9.1 %copy-start.10 = (bf16[384,1536]{1,0:T(8,128)(2,1)S(1)}, bf16[384,1536]{1,0:T(8,128)(2,1)}, u32[]{:S(2)}) copy-start(bf16[384,1536]{1,0:T(8,128)(2,1)} %copy-done.9) | copy-start | bytes 3538948
  342.5 20.1 %all-to-all-start.5 = ((bf16[1,8,48]{2,0,1:T(2,128)(2,1)}), bf16[1,8,48]{2,0,1:T(2,128)(2,1)S(1)}, u32[]{:S(2)}, u32[]{:S(2)}) async-start(bf16[1,8,48]{2,0,1:T(2,128)(2,1)} %convert_element_type.105), calls=%async_computation.5 | async-start | bytes 8192 | tf_op jit(solution)/shard_map/all_to_all | solution.py:136
  362.5 29.8 %all-to-all-start.4 = ((bf16[1,8,48,2560]{3,2,0,1:T(8,128)(2,1)}), bf16[1,8,48,2560]{3,2,0,1:T(8,128)(2,1)S(1)}, u32[]{:S(2)}, u32[]{:S(2)}) async-start(bf16[1,8,48,2560]{3,2,0,1:T(8,128)(2,1)} %bitcast.84), calls=%async_computation.4 | async-start | bytes 3932160 | tf_op jit(solution)/shard_map/all_to_all | solution.py:129
  397.9 55.8 %copy-start.3 = (f32[1,160,1536]{2,1,0:T(8,128)S(1)}, f32[1,160,1536]{2,1,0:T(8,128)}, u32[]{:S(2)}) copy-start(f32[1,160,1536]{2,1,0:T(8,128)} %param.18) | copy-start | bytes 2949124
  402.3 51.4 %copy-start.4 = (f32[1,160,1536]{2,1,0:T(8,128)S(1)}, f32[1,160,1536]{2,1,0:T(8,128)}, u32[]{:S(2)}) copy-start(f32[1,160,1536]{2,1,0:T(8,128)} %param.17) | copy-start | bytes 2949124
  453.7 5.8 %copy-start.1 = (bf16[128,2560]{1,0:T(8,128)(2,1)S(1)}, bf16[128,2560]{1,0:T(8,128)(2,1)}, u32[]{:S(2)}) copy-start(bf16[128,2560]{1,0:T(8,128)(2,1)} %param.13) | copy-start | bytes 1966084
Sparse Core Ops, SparseCore 0:
  11.0 108.9 all-gather.1
  142.9 82.3 reduce-scatter.4
  341.9 110.3 reduce-scatter.2
